TPU v7x, 128 devices: a whole 4x4x4 slice. The times are simulated.
128 devices in a mesh: seq: 32 (over x, y, core), tp: 4 (over z).
Axes of the slice: x: 4, y: 4, z: 4, core: 2. Of those that a mesh axis runs over, the one named last changes fastest.
Arguments:
- inputs: float32 [8192, 1024], P('seq', 'tp'), may hold values from -6 to 6
- cotangent: float32 [8192, 1024], P('seq', 'tp'), may hold values from -6 to 6
- entry_weight: float32 [2, 3, 1024, 1024], P(None, None, 'seq', 'tp'), may hold values from -0.1875 to 0.1875
- exit_weight: float32 [2, 1024, 1024], P(None, 'tp', 'seq'), may hold values from -0.1875 to 0.1875
- gate_up: float32 [2, 2, 1024, 4608], P(None, None, 'seq', 'tp'), may hold values from -0.1875 to 0.1875
- down_weight: float32 [2, 4608, 1024], P(None, 'tp', 'seq'), may hold values from -0.1875 to 0.1875
- conv_kernel: float32 [2, 3, 1024], P(None, None, 'tp'), may hold values from -3 to 3
- norm_gain: float32 [2, 2, 1024], P(None, None, 'tp'), may hold values from 0.5 to 1.5
- entry_first: float32 [2, 3, 1024, 1024], P(None, None, 'seq', 'tp'), may hold values from -27.1529 to 27.1529
- entry_second: float32 [2, 3, 1024, 1024], P(None, None, 'seq', 'tp'), may hold values from 0.8192 to 16.384
- exit_first: float32 [2, 1024, 1024], P(None, 'tp', 'seq'), may hold values from -27.1529 to 27.1529
- exit_second: float32 [2, 1024, 1024], P(None, 'tp', 'seq'), may hold values from 0.8192 to 16.384
- gate_first: float32 [2, 2, 1024, 4608], P(None, None, 'seq', 'tp'), may hold values from -27.1529 to 27.1529
- gate_second: float32 [2, 2, 1024, 4608], P(None, None, 'seq', 'tp'), may hold values from 0.8192 to 16.384
- down_first: float32 [2, 4608, 1024], P(None, 'tp', 'seq'), may hold values from -27.1529 to 27.1529
- down_second: float32 [2, 4608, 1024], P(None, 'tp', 'seq'), may hold values from 0.8192 to 16.384
- kernel_first: float32 [2, 3, 1024], P(None, None, 'tp'), may hold values from -27.1529 to 27.1529
- kernel_second: float32 [2, 3, 1024], P(None, None, 'tp'), may hold values from 0.8192 to 16.384
- gain_first: float32 [2, 2, 1024], P(None, None, 'tp'), may hold values from -27.1529 to 27.1529
- gain_second: float32 [2, 2, 1024], P(None, None, 'tp'), may hold values from 0.8192 to 16.384
Outputs:
- output: float32 [8192, 1024], P('seq', 'tp')
- input_grad: float32 [8192, 1024], P('seq', 'tp')
- entry_grad: float32 [2, 3, 1024, 1024], P(None, None, 'seq', 'tp')
- exit_grad: float32 [2, 1024, 1024], P(None, 'tp', 'seq')
- gate_grad: float32 [2, 2, 1024, 4608], P(None, None, 'seq', 'tp')
- down_grad: float32 [2, 4608, 1024], P(None, 'tp', 'seq')
- kernel_grad: float32 [2, 3, 1024], P(None, None, 'tp')
- gain_grad: float32 [2, 2, 1024], P(None, None, 'tp')
- entry_updated: float32 [2, 3, 1024, 1024], P(None, None, 'seq', 'tp')
- exit_updated: float32 [2, 1024, 1024], P(None, 'tp', 'seq')
- gate_updated: float32 [2, 2, 1024, 4608], P(None, None, 'seq', 'tp')
- down_updated: float32 [2, 4608, 1024], P(None, 'tp', 'seq')
- kernel_updated: float32 [2, 3, 1024], P(None, None, 'tp')
- gain_updated: float32 [2, 2, 1024], P(None, None, 'tp')
- entry_first_new: float32 [2, 3, 1024, 1024], P(None, None, 'seq', 'tp')
- entry_second_new: float32 [2, 3, 1024, 1024], P(None, None, 'seq', 'tp')
- exit_first_new: float32 [2, 1024, 1024], P(None, 'tp', 'seq')
- exit_second_new: float32 [2, 1024, 1024], P(None, 'tp', 'seq')
- gate_first_new: float32 [2, 2, 1024, 4608], P(None, None, 'seq', 'tp')
- gate_second_new: float32 [2, 2, 1024, 4608], P(None, None, 'seq', 'tp')
- down_first_new: float32 [2, 4608, 1024], P(None, 'tp', 'seq')
- down_second_new: float32 [2, 4608, 1024], P(None, 'tp', 'seq')
- kernel_first_new: float32 [2, 3, 1024], P(None, None, 'tp')
- kernel_second_new: float32 [2, 3, 1024], P(None, None, 'tp')
- gain_first_new: float32 [2, 2, 1024], P(None, None, 'tp')
- gain_second_new: float32 [2, 2, 1024], P(None, None, 'tp')
All inputs are finite; a program needn't handle non-finite values.
Results may differ from a plain program's by a relative error of at most 0.019.
The roundings to bfloat16 on the way count: a program that leaves them out, or rounds other values in their place, can miss the bound.
Values may be sent and summed in bfloat16 or wider, within the bound.
A program may use at most 192 MiB of HBM per device.

v0:
```python
import jax
import jax.numpy as jnp
from jax import lax
from jax.sharding import PartitionSpec as P

STEP = 4
EPS = 1e-06


def from_everyone(value, axis):
    copies = jnp.broadcast_to(value, (lax.axis_size(axis), *value.shape))
    return lax.all_to_all(copies, axis, split_axis=0, concat_axis=0, tiled=True)


def taken_together(value, axis):
    return from_everyone(value, axis).sum(axis=0)


def joined_along(blocks, dim):
    blocks = jnp.moveaxis(blocks, 0, dim)
    dims = blocks.shape
    return blocks.reshape(*dims[:dim], dims[dim] * dims[dim + 1], *dims[dim + 2 :])


def collect(value, axis, dim):
    return joined_along(from_everyone(value, axis), dim)


def cut_along(value, dim, peers):
    dims = value.shape
    blocks = value.reshape(*dims[:dim], peers, dims[dim] // peers, *dims[dim + 1 :])
    return jnp.moveaxis(blocks, dim, 0)


def sent_and_summed(value, axis, dim):
    peers = lax.axis_size(axis)
    blocks = lax.all_to_all(cut_along(value, dim, peers), axis, 0, 0, tiled=True)
    return jnp.sum(blocks, axis=0)


def from_behind(value, axis, by):
    peers = lax.axis_size(axis)
    pairs = [(i, i + by) for i in range(peers) if 0 <= i + by < peers]
    return lax.ppermute(value, axis, pairs)


def gather_turned(arrays, axis, dims):
    turned = [jnp.moveaxis(a, dim, 0) for a, dim in zip(arrays, dims)]
    widths = [t[0].size for t in turned]
    both = jnp.concatenate([t.reshape(-1, w) for t, w in zip(turned, widths)], axis=1)
    out = lax.all_gather(both, axis, axis=0, tiled=True)
    blocks = jnp.split(out, [sum(widths[:k]) for k in range(1, len(widths))], axis=1)
    return tuple(
        (
            jnp.moveaxis(b.reshape(-1, *t.shape[1:]), 0, dim)
            for b, t, dim in zip(blocks, turned, dims)
        )
    )


def packed_total(arrays, axis):
    ravelled, at, done = (jnp.concatenate([a.reshape(-1) for a in arrays]), 0, [])
    running = taken_together(ravelled, axis)
    for a in arrays:
        done.append(running[at : at + a.size].reshape(a.shape))
        at += a.size
    return tuple(done)


def bdot(left, right):
    return jnp.dot(left, right, preferred_element_type=jnp.float32)


def row_norm(value, width):
    sums = taken_together(jnp.sum(value * value, axis=1), "tp")
    scale = lax.rsqrt(sums / width + EPS)[:, None]
    return (value * scale, scale)


def norm_back(dnorm, normed, scale, gain, width):
    dnormed = dnorm * gain
    inner = taken_together(jnp.sum(dnormed * normed, axis=1), "tp")
    return (scale * (dnormed - normed * (inner / width)[:, None]), jnp.sum(dnorm * normed, axis=0))


def whole_rows(shard):
    return collect(shard, "tp", 1)


def whole_grads(shard):
    return collect(shard, "tp", 1)


def channel_sum(partial_value):
    return sent_and_summed(partial_value, "tp", 1)


def adamw(weight, grad, first, second, rate, decay):
    first_new = 0.9 * first + 0.1 * grad
    second_new = 0.999 * second + 0.001 * grad * grad
    update = first_new / (1.0 - 0.9**STEP) / (jnp.sqrt(second_new / (1.0 - 0.999**STEP)) + 1e-08)
    return (weight - rate * (update + decay * weight), first_new, second_new)


def layer_forward(hidden, entry, leave, gates, down, kern, gain, width):
    normed1, scale1 = row_norm(hidden, width)
    first_in = whole_rows((normed1 * gain[0]).astype(jnp.bfloat16))
    projected = jnp.einsum("td,cde->cte", first_in, entry, preferred_element_type=jnp.float32)
    b_part, c_part, x_part = (projected[0], projected[1], projected[2])
    product = b_part * x_part
    before = from_behind(product[-2:], "seq", 1)
    extended = jnp.concatenate([before, product], axis=0)
    conv_out = kern[0] * extended[:-2] + kern[1] * extended[1:-1] + kern[2] * extended[2:]
    gated = (c_part * conv_out).astype(jnp.bfloat16)
    mid = hidden + channel_sum(bdot(gated, leave))
    normed2, scale2 = row_norm(mid, width)
    second_in = whole_rows((normed2 * gain[1]).astype(jnp.bfloat16))
    gate_val = bdot(second_in, gates[0])
    up_val = bdot(second_in, gates[1])
    sig = jax.nn.sigmoid(gate_val)
    swish = gate_val * sig
    acted = (swish * up_val).astype(jnp.bfloat16)
    result = mid + channel_sum(bdot(acted, down))
    kept = (
        normed1,
        scale1,
        first_in,
        b_part,
        c_part,
        x_part,
        extended,
        conv_out,
        gated,
        normed2,
        scale2,
        second_in,
        gate_val,
        up_val,
        sig,
        swish,
        acted,
    )
    return (result, kept)


def layer_backward(grad, kept, entry, leave, gates, down, kern, gain, width):
    (
        normed1,
        scale1,
        first_in,
        b_part,
        c_part,
        x_part,
        extended,
        conv_out,
        gated,
        normed2,
        scale2,
        second_in,
        gate_val,
        up_val,
        sig,
        swish,
        acted,
    ) = kept
    grad_rows = whole_grads(grad.astype(jnp.bfloat16))
    dacted = bdot(grad_rows, down.T)
    down_g = bdot(acted.T, grad_rows)
    dgate = (dacted * up_val * sig * (1.0 + gate_val * (1.0 - sig))).astype(jnp.bfloat16)
    dup = (dacted * swish).astype(jnp.bfloat16)
    gate_g = jnp.stack([bdot(second_in.T, dgate), bdot(second_in.T, dup)])
    dnorm2 = channel_sum(bdot(dgate, gates[0].T) + bdot(dup, gates[1].T))
    back2, dgain2 = norm_back(dnorm2, normed2, scale2, gain[1], width)
    dmid = grad + back2
    mid_rows = whole_grads(dmid.astype(jnp.bfloat16))
    dgated = bdot(mid_rows, leave.T)
    exit_g = bdot(gated.T, mid_rows)
    dc_part = dgated * conv_out
    dconv = dgated * c_part
    kernel_g = jnp.stack(
        [
            jnp.sum(dconv * extended[:-2], axis=0),
            jnp.sum(dconv * extended[1:-1], axis=0),
            jnp.sum(dconv * extended[2:], axis=0),
        ]
    )
    channels = dconv.shape[1]
    zero_one = jnp.zeros((1, channels), jnp.float32)
    zero_two = jnp.zeros((2, channels), jnp.float32)
    dextended = (
        jnp.concatenate([kern[0] * dconv, zero_two], axis=0)
        + jnp.concatenate([zero_one, kern[1] * dconv, zero_one], axis=0)
        + jnp.concatenate([zero_two, kern[2] * dconv], axis=0)
    )
    returned = from_behind(dextended[:2], "seq", -1)
    tokens = dconv.shape[0]
    dproduct = dextended[2:] + jnp.concatenate(
        [jnp.zeros((tokens - 2, channels), jnp.float32), returned], axis=0
    )
    dproj = jnp.stack([dproduct * x_part, dc_part, dproduct * b_part]).astype(jnp.bfloat16)
    entry_g = jnp.einsum("td,cte->cde", first_in, dproj, preferred_element_type=jnp.float32)
    dnorm1 = channel_sum(
        jnp.einsum("cte,cde->td", dproj, entry, preferred_element_type=jnp.float32)
    )
    back1, dgain1 = norm_back(dnorm1, normed1, scale1, gain[0], width)
    return (dmid + back1, (entry_g, exit_g, gate_g, down_g), kernel_g, jnp.stack([dgain1, dgain2]))


def per_device(
    inputs,
    cotangent,
    entry_weight,
    exit_weight,
    gate_up,
    down_weight,
    conv_kernel,
    norm_gain,
    entry_first,
    entry_second,
    exit_first,
    exit_second,
    gate_first,
    gate_second,
    down_first,
    down_second,
    kernel_first,
    kernel_second,
    gain_first,
    gain_second,
):
    width = inputs.shape[1] * lax.axis_size("tp")
    layers = entry_weight.shape[0]
    rounded = (
        entry_weight.astype(jnp.bfloat16),
        exit_weight.astype(jnp.bfloat16),
        gate_up.astype(jnp.bfloat16),
        down_weight.astype(jnp.bfloat16),
    )
    gathered = gather_turned((rounded[0], rounded[1], rounded[2], rounded[3]), "seq", (2, 2, 2, 2))
    hidden = inputs
    kept_all = []
    for layer in range(layers):
        hidden, kept = layer_forward(
            hidden,
            gathered[0][layer],
            gathered[1][layer],
            gathered[2][layer],
            gathered[3][layer],
            conv_kernel[layer],
            norm_gain[layer],
            width,
        )
        kept_all.append(kept)
    grad = cotangent
    matrix_terms = [None] * layers
    kernel_terms = [None] * layers
    gain_terms = [None] * layers
    for layer in reversed(range(layers)):
        grad, terms, kernel_g, gain_g = layer_backward(
            grad,
            kept_all[layer],
            gathered[0][layer],
            gathered[1][layer],
            gathered[2][layer],
            gathered[3][layer],
            conv_kernel[layer],
            norm_gain[layer],
            width,
        )
        matrix_terms[layer] = terms
        kernel_terms[layer] = kernel_g
        gain_terms[layer] = gain_g
    stacked = tuple(
        (jnp.stack([matrix_terms[layer][index] for layer in range(layers)]) for index in range(4))
    )
    summed = lax.psum_scatter(stacked, "seq", scatter_dimension=2, tiled=True)
    kernel_grad, gain_grad = packed_total((jnp.stack(kernel_terms), jnp.stack(gain_terms)), "seq")
    entry_grad, exit_grad, gate_grad, down_grad = summed
    entry_u, entry_f, entry_s = adamw(
        entry_weight, entry_grad, entry_first, entry_second, 0.01, 0.1
    )
    exit_u, exit_f, exit_s = adamw(exit_weight, exit_grad, exit_first, exit_second, 0.01, 0.1)
    gate_u, gate_f, gate_s = adamw(gate_up, gate_grad, gate_first, gate_second, 0.01, 0.1)
    down_u, down_f, down_s = adamw(down_weight, down_grad, down_first, down_second, 0.01, 0.1)
    kernel_u, kernel_f, kernel_s = adamw(
        conv_kernel, kernel_grad, kernel_first, kernel_second, 0.2, 0.0
    )
    gain_u, gain_f, gain_s = adamw(norm_gain, gain_grad, gain_first, gain_second, 0.2, 0.0)
    return (
        hidden,
        grad,
        entry_grad,
        exit_grad,
        gate_grad,
        down_grad,
        kernel_grad,
        gain_grad,
        entry_u,
        exit_u,
        gate_u,
        down_u,
        kernel_u,
        gain_u,
        entry_f,
        entry_s,
        exit_f,
        exit_s,
        gate_f,
        gate_s,
        down_f,
        down_s,
        kernel_f,
        kernel_s,
        gain_f,
        gain_s,
    )


def solution(mesh):
    placed = (
        P("seq", "tp"),
        P("seq", "tp"),
        P(None, None, "seq", "tp"),
        P(None, "tp", "seq"),
        P(None, None, "seq", "tp"),
        P(None, "tp", "seq"),
        P(None, None, "tp"),
        P(None, None, "tp"),
        P(None, None, "seq", "tp"),
        P(None, None, "seq", "tp"),
        P(None, "tp", "seq"),
        P(None, "tp", "seq"),
        P(None, None, "seq", "tp"),
        P(None, None, "seq", "tp"),
        P(None, "tp", "seq"),
        P(None, "tp", "seq"),
        P(None, None, "tp"),
        P(None, None, "tp"),
        P(None, None, "tp"),
        P(None, None, "tp"),
    )
    return jax.shard_map(
        per_device,
        mesh=mesh,
        in_specs=placed,
        out_specs=(
            P("seq", "tp"),
            P("seq", "tp"),
            P(None, None, "seq", "tp"),
            P(None, "tp", "seq"),
            P(None, None, "seq", "tp"),
            P(None, "tp", "seq"),
            P(None, None, "tp"),
            P(None, None, "tp"),
            P(None, None, "seq", "tp"),
            P(None, "tp", "seq"),
            P(None, None, "seq", "tp"),
            P(None, "tp", "seq"),
            P(None, None, "tp"),
            P(None, None, "tp"),
            P(None, None, "seq", "tp"),
            P(None, None, "seq", "tp"),
            P(None, "tp", "seq"),
            P(None, "tp", "seq"),
            P(None, None, "seq", "tp"),
            P(None, None, "seq", "tp"),
            P(None, "tp", "seq"),
            P(None, "tp", "seq"),
            P(None, None, "tp"),
            P(None, None, "tp"),
            P(None, None, "tp"),
            P(None, None, "tp"),
        ),
        check_vma=False,
    )
```

profile of v0, /device:TPU:0, one launch (start us, length us, event | category | flops | bytes accessed | tf_op | source)
XLA Modules:
  0.0 816.9 jit_solution(14901821055226626452)
XLA Ops:
  11.7 5.4 all-to-all-start
  17.2 5.2 all-to-all-done
  26.9 8.2 %all-to-all-done.1 = bf16[4,256,256]{2,1,0:T(8,128)(2,1)S(1)} async-done(((bf16[4,256,256]{2,1,0:T(8,128)(2,1)}), bf16[4,256,256]{2,1,0:T(8,128)(2,1)S(1)}, u32[]{:S(2)}, u32[]{:S(2)}) %all-to-all-start.1) | async-done | bytes 524320 | tf_op jit(solution)/shard_map/all_to_all | solution.py:12
  36.8 52.9 %all-gather.2.cloned.1.call-done = bf16[1024,8960]{1,0:T(8,128)(2,1)} async-done(((bf16[32,8960]{1,0:T(8,128)(2,1)}), bf16[1024,8960]{1,0:T(8,128)(2,1)}) %all-gather.2.cloned.1.call-update) | async-done | bytes 18350096 | tf_op jit(solution)/shard_map/all_gather | solution.py:51
  107.0 20.4 %all_to_all.134 = f32[4,256,256]{2,1,0:T(8,128)S(1)} all-to-all(f32[4,256,256]{2,1,0:T(8,128)S(1)} %convolution_bitcast_fusion.16), channel_id=1, replica_groups=mesh['seq'=32,'tp'=4] {'tp'}, dimensions={0} | all-to-all | bytes 2097152 | tf_op jit(solution)/shard_map/all_to_all | solution.py:37
  131.5 7.9 split.18
  139.4 13.0 %reshape.240 = bf16[1024,2,2,1152]{3,2,1,0:T(2,128)(2,1)} reshape(bf16[1024,4608]{1,0:T(8,128)(2,1)} %split.18) | data formatting | bytes 18874368 | tf_op jit(solution)/shard_map/reshape | solution.py:55
  152.5 8.5 %copy.432 = bf16[1024,2,2,1152]{3,0,2,1:T(8,128)(2,1)} copy(bf16[1024,2,2,1152]{3,2,1,0:T(2,128)(2,1)} %reshape.240) | data formatting | bytes 18874368 | tf_op jit(solution)/shard_map/reshape | solution.py:55
  165.7 6.6 copy.342
  194.9 17.7 %all_to_all.135 = f32[4,256,256]{2,1,0:T(8,128)S(1)} all-to-all(f32[4,256,256]{2,1,0:T(8,128)S(1)} %convolution_bitcast_fusion.15), channel_id=1, replica_groups=mesh['seq'=32,'tp'=4] {'tp'}, dimensions={0} | all-to-all | bytes 2097152 | tf_op jit(solution)/shard_map/all_to_all | solution.py:37
  212.8 7.6 all_to_all.136
  220.6 10.9 %all_to_all.137 = bf16[4,256,256]{2,1,0:T(8,128)(2,1)S(1)} all-to-all(bf16[4,256,256]{2,1,0:T(8,128)(2,1)S(1)} %broadcast_in_dim.64), channel_id=1, replica_groups=mesh['seq'=32,'tp'=4] {'tp'}, dimensions={0} | all-to-all | bytes 1048576 | tf_op jit(solution)/shard_map/all_to_all | solution.py:12
  238.2 18.5 %all_to_all.138 = f32[4,256,256]{2,1,0:T(8,128)S(1)} all-to-all(f32[4,256,256]{2,1,0:T(8,128)S(1)} %convolution_bitcast_fusion.14), channel_id=1, replica_groups=mesh['seq'=32,'tp'=4] {'tp'}, dimensions={0} | all-to-all | bytes 2097152 | tf_op jit(solution)/shard_map/all_to_all | solution.py:37
  256.9 7.6 all_to_all.139
  269.2 8.9 %all-to-all-done.10 = bf16[4,256,256]{1,2,0:T(8,128)(2,1)S(1)} async-done(((bf16[4,256,256]{1,2,0:T(8,128)(2,1)}), bf16[4,256,256]{1,2,0:T(8,128)(2,1)S(1)}, u32[]{:S(2)}, u32[]{:S(2)}) %all-to-all-start.10) | async-done | bytes 524320 | tf_op jit(solution)/shard_map/all_to_all | solution.py:12
  311.6 6.4 all-to-all-done.13
  323.6 9.0 %all-to-all-done.11 = f32[4,256,256]{2,1,0:T(8,128)S(1)} async-done(((f32[4,256,256]{2,1,0:T(8,128)}), f32[4,256,256]{2,1,0:T(8,128)S(1)}, u32[]{:S(2)}, u32[]{:S(2)}) %all-to-all-start.11) | async-done | bytes 1048608 | tf_op jit(solution)/shard_map/all_to_all | solution.py:37
  343.9 10.5 %all_to_all.140 = bf16[4,256,256]{1,2,0:T(8,128)(2,1)S(1)} all-to-all(bf16[4,256,256]{1,2,0:T(8,128)(2,1)S(1)} %broadcast_in_dim.69), channel_id=1, replica_groups=mesh['seq'=32,'tp'=4] {'tp'}, dimensions={0} | all-to-all | bytes 1048576 | tf_op jit(solution)/shard_map/all_to_all | solution.py:12
  361.4 19.6 %all_to_all.141 = f32[4,256,256]{2,1,0:T(8,128)} all-to-all(f32[4,256,256]{2,1,0:T(8,128)S(1)} %convolution_bitcast_fusion.10), channel_id=1, replica_groups=mesh['seq'=32,'tp'=4] {'tp'}, dimensions={0} | all-to-all | bytes 2097152 | tf_op jit(solution)/shard_map/all_to_all | solution.py:37
  383.0 7.6 all_to_all.142
  392.4 11.2 %all_to_all.143 = bf16[4,256,256]{1,2,0:T(8,128)(2,1)S(1)} all-to-all(bf16[4,256,256]{1,2,0:T(8,128)(2,1)S(1)} %broadcast_in_dim.71), channel_id=1, replica_groups=mesh['seq'=32,'tp'=4] {'tp'}, dimensions={0} | all-to-all | bytes 1048576 | tf_op jit(solution)/shard_map/all_to_all | solution.py:12
  426.2 5.6 all-to-all-done.19
  448.3 9.4 %pad_maximum_fusion.1 = f32[2,1152,1024]{2,1,0:T(8,128)} fusion(f32[1,1152,1024]{2,1,0:T(8,128)} %convolution_bitcast_fusion, f32[1,1152,1024]{2,1,0:T(8,128)} %convolution_bitcast_fusion.1), kind=kLoop, calls=%fused_computation.3 | loop fusion | flops 2359296 | bytes 18874368 | tf_op jit(solution)/shard_map/stack | solution.py:274
  457.6 14.9 %copy.367 = f32[2,1152,1024]{1,0,2:T(2,128)} copy(f32[2,1152,1024]{2,1,0:T(8,128)} %pad_maximum_fusion.1) | data formatting | bytes 18874368 | tf_op jit(solution)/shard_map/stack | solution.py:274
  486.0 10.4 %copy.365 = f32[2,3,1024,256]{3,0,1,2:T(2,128)} copy(f32[2,3,1024,256]{2,3,1,0:T(8,128)} %pad_maximum_fusion.2) | data formatting | bytes 12582912 | tf_op jit(solution)/shard_map/stack | solution.py:274
  510.3 6.9 pad_maximum_fusion
  526.6 15.0 %all-to-all-done.22 = f32[4,256,256]{2,1,0:T(8,128)S(1)} async-done(((f32[4,256,256]{2,1,0:T(8,128)}), f32[4,256,256]{2,1,0:T(8,128)S(1)}, u32[]{:S(2)}, u32[]{:S(2)}) %all-to-all-start.22) | async-done | bytes 1048608 | tf_op jit(solution)/shard_map/all_to_all | solution.py:37
  545.9 5.2 all-to-all-done.23
  552.1 5.7 all-to-all-start.24
  558.7 9.7 %all-to-all-done.24 = f32[32,1,2560]{2,1,0:T(1,128)S(1)} async-done(((f32[32,1,2560]{2,1,0:T(1,128)}), f32[32,1,2560]{2,1,0:T(1,128)S(1)}, u32[]{:S(2)}, u32[]{:S(2)}) %all-to-all-start.24) | async-done | bytes 327712 | tf_op jit(solution)/shard_map/all_to_all | solution.py:12
  571.7 109.6 %all-reduce.12.cloned.1.call-done = (f32[2,3,1024,256]{3,0,1,2:T(2,128)}, f32[2,256,1024]{1,0,2:T(2,128)}, f32[2,1152,1024]{1,0,2:T(2,128)}) async-done(((f32[2,3,1024,256]{3,0,1,2:T(2,128)}, f32[2,256,1024]{1,0,2:T(2,128)}, f32[2,1152,1024]{1,0,2:T(2,128)}), (f32[2,3,1024,256]{3,0,1,2:T(2,128)}, f32[2,256,1024]{1,0,2:T(2,128)}, f32[2,1152,1024]{1,0,2:T(2,128)})) %all-reduce.12.cloned.1.call-update) | async-done | bytes 17825808
  686.9 120.7 %reduce-scatter.2.cloned.1.call-done = f32[2,2,32,1152]{3,2,1,0:T(8,128)} async-done(((f32[2,2,1024,1152]{3,2,1,0:T(8,128)}), f32[2,2,32,1152]{3,2,1,0:T(8,128)}) %reduce-scatter.2.cloned.1.call-update) | async-done | bytes 589840 | tf_op jit(solution)/shard_map/reduce_scatter | solution.py:276
  (418 shorter events, 223.6 us)
Async XLA Ops:
  7.2 82.4 %all-gather.2.cloned.1.call-start = ((), (), s32[]{:S(2)}) async-start(), calls=%async_computation.26 | async-start | bytes 18923520 | tf_op jit(solution)/shard_map/all_gather | solution.py:51
  11.7 10.7 %all-to-all-start = ((f32[4,1,256]{2,1,0:T(1,128)}), f32[4,1,256]{2,1,0:T(1,128)S(1)}, u32[]{:S(2)}, u32[]{:S(2)}) async-start(f32[4,1,256]{2,1,0:T(1,128)} %broadcast_in_dim.59), calls=%async_computation | async-start | bytes 8192 | tf_op jit(solution)/shard_map/all_to_all | solution.py:12
  17.1 155.3 %copy-start.78 = (f32[1,1,256]{2,1,0:T(1,128)}, f32[1,1,256]{2,1,0:T(1,128)S(1)}, u32[]{:S(2)}) copy-start(f32[1,1,256]{2,1,0:T(1,128)S(1)} %get-tuple-element.270) | copy-start | bytes 3076
  17.2 365.2 %copy-start.80 = (f32[1,1,256]{2,1,0:T(1,128)}, f32[1,1,256]{2,1,0:T(1,128)S(1)}, u32[]{:S(2)}) copy-start(f32[1,1,256]{2,1,0:T(1,128)S(1)} %get-tuple-element.269) | copy-start | bytes 3076
  23.4 11.8 %all-to-all-start.1 = ((bf16[4,256,256]{2,1,0:T(8,128)(2,1)}), bf16[4,256,256]{2,1,0:T(8,128)(2,1)S(1)}, u32[]{:S(2)}, u32[]{:S(2)}) async-start(bf16[4,256,256]{2,1,0:T(8,128)(2,1)} %broadcast_in_dim.60), calls=%async_computation.1 | async-start | bytes 1048576 | tf_op jit(solution)/shard_map/all_to_all | solution.py:12
  101.3 3.9 collective-permute-start
  128.3 44.1 %all-to-all-start.3 = ((f32[4,1,256]{2,1,0:T(1,128)}), f32[4,1,256]{2,1,0:T(1,128)S(1)}, u32[]{:S(2)}, u32[]{:S(2)}) async-start(f32[4,1,256]{2,1,0:T(1,128)} %broadcast_in_dim.61), calls=%async_computation.3 | async-start | bytes 8192 | tf_op jit(solution)/shard_map/all_to_all | solution.py:12
  173.5 14.0 %all-to-all-start.4 = ((bf16[4,256,256]{1,2,0:T(8,128)(2,1)}), bf16[4,256,256]{1,2,0:T(8,128)(2,1)S(1)}, u32[]{:S(2)}, u32[]{:S(2)}) async-start(bf16[4,256,256]{1,2,0:T(8,128)(2,1)} %broadcast_in_dim.62), calls=%async_computation.4 | async-start | bytes 1048576 | tf_op jit(solution)/shard_map/all_to_all | solution.py:12
  234.6 2.1 collective-permute-start.1
  265.6 12.5 %all-to-all-start.10 = ((bf16[4,256,256]{1,2,0:T(8,128)(2,1)}), bf16[4,256,256]{1,2,0:T(8,128)(2,1)S(1)}, u32[]{:S(2)}, u32[]{:S(2)}) async-start(bf16[4,256,256]{1,2,0:T(8,128)(2,1)} %broadcast_in_dim.66), calls=%async_computation.10 | async-start | bytes 1048576 | tf_op jit(solution)/shard_map/all_to_all | solution.py:12
  278.9 11.5 %all-to-all-start.12 = ((bf16[4,256,256]{1,2,0:T(8,128)(2,1)}), bf16[4,256,256]{1,2,0:T(8,128)(2,1)S(1)}, u32[]{:S(2)}, u32[]{:S(2)}) async-start(bf16[4,256,256]{1,2,0:T(8,128)(2,1)} %broadcast_in_dim.67), calls=%async_computation.12 | async-start | bytes 1048576 | tf_op jit(solution)/shard_map/all_to_all | solution.py:12
  301.4 16.6 %all-to-all-start.13 = ((f32[4,256,256]{2,1,0:T(8,128)}), f32[4,256,256]{2,1,0:T(8,128)}, u32[]{:S(2)}, u32[]{:S(2)}) async-start(f32[4,256,256]{2,1,0:T(8,128)} %bitcast.334), calls=%async_computation.13 | async-start | bytes 2097152 | tf_op jit(solution)/shard_map/all_to_all | solution.py:37
  318.0 14.6 %all-to-all-start.11 = ((f32[4,256,256]{2,1,0:T(8,128)}), f32[4,256,256]{2,1,0:T(8,128)S(1)}, u32[]{:S(2)}, u32[]{:S(2)}) async-start(f32[4,256,256]{2,1,0:T(8,128)} %convolution_bitcast_fusion.13), calls=%async_computation.11 | async-start | bytes 2097152 | tf_op jit(solution)/shard_map/all_to_all | solution.py:37
  333.2 8.5 %all-to-all-start.14 = ((f32[4,1,256]{2,1,0:T(1,128)}), f32[4,1,256]{2,1,0:T(1,128)S(1)}, u32[]{:S(2)}, u32[]{:S(2)}) async-start(f32[4,1,256]{2,1,0:T(1,128)} %broadcast_in_dim.68), calls=%async_computation.14 | async-start | bytes 8192 | tf_op jit(solution)/shard_map/all_to_all | solution.py:12
  356.8 3.2 collective-permute-start.2
  414.0 17.7 %all-to-all-start.19 = ((f32[4,256,256]{2,1,0:T(8,128)}), f32[4,256,256]{2,1,0:T(8,128)}, u32[]{:S(2)}, u32[]{:S(2)}) async-start(f32[4,256,256]{2,1,0:T(8,128)} %bitcast.369), calls=%async_computation.19 | async-start | bytes 2097152 | tf_op jit(solution)/shard_map/all_to_all | solution.py:37
  434.4 8.5 %all-to-all-start.20 = ((f32[4,1,256]{2,1,0:T(1,128)}), f32[4,1,256]{2,1,0:T(1,128)S(1)}, u32[]{:S(2)}, u32[]{:S(2)}) async-start(f32[4,1,256]{2,1,0:T(1,128)} %broadcast_in_dim.72), calls=%async_computation.20 | async-start | bytes 8192 | tf_op jit(solution)/shard_map/all_to_all | solution.py:12
  444.7 27.8 %all-to-all-start.21 = ((bf16[4,256,256]{1,2,0:T(8,128)(2,1)}), bf16[4,256,256]{1,2,0:T(8,128)(2,1)S(1)}, u32[]{:S(2)}, u32[]{:S(2)}) async-start(bf16[4,256,256]{1,2,0:T(8,128)(2,1)} %broadcast_in_dim.73), calls=%async_computation.21 | async-start | bytes 1048576 | tf_op jit(solution)/shard_map/all_to_all | solution.py:12
  448.3 233.0 %all-reduce.12.cloned.1.call-start = ((), (), s32[]{:S(2)}) async-start(), calls=%async_computation.28 | async-start | bytes 35651584
  475.9 3.9 collective-permute-start.3
  496.4 311.2 %reduce-scatter.2.cloned.1.call-start = ((), (), s32[]{:S(2)}) async-start(), calls=%async_computation.27 | async-start | bytes 19464192 | tf_op jit(solution)/shard_map/reduce_scatter | solution.py:276
  520.3 21.3 %all-to-all-start.22 = ((f32[4,256,256]{2,1,0:T(8,128)}), f32[4,256,256]{2,1,0:T(8,128)S(1)}, u32[]{:S(2)}, u32[]{:S(2)}) async-start(f32[4,256,256]{2,1,0:T(8,128)} %convolution_bitcast_fusion.9), calls=%async_computation.22 | async-start | bytes 2097152 | tf_op jit(solution)/shard_map/all_to_all | solution.py:37
  541.7 142.3 %copy-start.65 = (f32[2,256,32]{1,2,0:T(8,128)S(1)}, f32[2,256,32]{1,2,0:T(8,128)}, u32[]{:S(2)}) copy-start(f32[2,256,32]{1,2,0:T(8,128)} %param.23) | copy-start | bytes 196612
  541.7 142.3 %copy-start.68 = (f32[2,256,32]{1,2,0:T(8,128)S(1)}, f32[2,256,32]{1,2,0:T(8,128)}, u32[]{:S(2)}) copy-start(f32[2,256,32]{1,2,0:T(8,128)} %param.30) | copy-start | bytes 196612
  541.8 142.3 %copy-start.69 = (f32[2,256,32]{1,2,0:T(8,128)S(1)}, f32[2,256,32]{1,2,0:T(8,128)}, u32[]{:S(2)}) copy-start(f32[2,256,32]{1,2,0:T(8,128)} %param.31) | copy-start | bytes 196612
  541.8 143.1 %copy-start.49 = (f32[2,3,32,256]{3,2,1,0:T(8,128)S(1)}, f32[2,3,32,256]{3,2,1,0:T(8,128)}, u32[]{:S(2)}) copy-start(f32[2,3,32,256]{3,2,1,0:T(8,128)} %param.22) | copy-start | bytes 589828
  541.8 143.0 %copy-start.66 = (f32[2,3,32,256]{3,2,1,0:T(8,128)S(1)}, f32[2,3,32,256]{3,2,1,0:T(8,128)}, u32[]{:S(2)}) copy-start(f32[2,3,32,256]{3,2,1,0:T(8,128)} %param.28) | copy-start | bytes 589828
  541.8 143.0 %copy-start.67 = (f32[2,3,32,256]{3,2,1,0:T(8,128)S(1)}, f32[2,3,32,256]{3,2,1,0:T(8,128)}, u32[]{:S(2)}) copy-start(f32[2,3,32,256]{3,2,1,0:T(8,128)} %param.29) | copy-start | bytes 589828
  542.7 8.5 %all-to-all-start.23 = ((f32[4,1,256]{2,1,0:T(1,128)}), f32[4,1,256]{2,1,0:T(1,128)S(1)}, u32[]{:S(2)}, u32[]{:S(2)}) async-start(f32[4,1,256]{2,1,0:T(1,128)} %broadcast_in_dim.74), calls=%async_computation.23 | async-start | bytes 8192 | tf_op jit(solution)/shard_map/all_to_all | solution.py:12
  552.1 16.3 %all-to-all-start.24 = ((f32[32,1,2560]{2,1,0:T(1,128)}), f32[32,1,2560]{2,1,0:T(1,128)S(1)}, u32[]{:S(2)}, u32[]{:S(2)}) async-start(f32[32,1,2560]{2,1,0:T(1,128)} %broadcast_in_dim.75), calls=%async_computation.25 | async-start | bytes 655360 | tf_op jit(solution)/shard_map/all_to_all | solution.py:12
  557.8 128.0 %copy-start.37 = (f32[2,1152,32]{1,2,0:T(8,128)S(1)}, f32[2,1152,32]{1,2,0:T(8,128)}, u32[]{:S(2)}) copy-start(f32[2,1152,32]{1,2,0:T(8,128)} %param.25) | copy-start | bytes 884740
  557.8 128.0 %copy-start.62 = (f32[2,1152,32]{1,2,0:T(8,128)S(1)}, f32[2,1152,32]{1,2,0:T(8,128)}, u32[]{:S(2)}) copy-start(f32[2,1152,32]{1,2,0:T(8,128)} %param.34) | copy-start | bytes 884740
  (97 other events, 1976.2 us)
Sparse Core Ops, SparseCore 0:
  11.1 78.4 all-gather.1
  496.5 184.7 all-reduce.11
  685.8 121.7 reduce-scatter.1
where the time goes:
time: 829 us; the launch traced here: 817 us
  waiting for transfers between devices  366 us (44%)
  blocking collectives  132 us (16%)
  local copies, waits for them, and re-layouts  117 us (14%)
  starting transfers between devices  66.1 us (8%)
  matrix products  64.9 us (8%)
  other arithmetic  54.2 us (7%)
  between operations  16.5 us (2%)
    reduce_scatter x1, waiting for transfers between devices, per_device(): summed = lax.psum_scatter(stacked, 'seq', scatter_dimension=2, tiled=True)  121 us
    unnamed x4, waiting for transfers between devices  110 us
    all_to_all x4, blocking collectives, sent_and_summed(): lax.all_to_all(cut_along(value, dim, peers), axis, 0, 0, tiled=True)  76.1 us
    all_to_all x6, blocking collectives, from_everyone(): return lax.all_to_all(copies, axis, split_axis=0, concat_axis=0, tiled=True)  55.5 us
    dot_general x24, matrix products, bdot(): return jnp.dot(left, right, preferred_element_type=jnp.float32)  54.6 us
    all_gather x1, waiting for transfers between devices, gather_turned(): out = lax.all_gather(both, axis, axis=0, tiled=True)  52.9 us
    all_to_all x11, waiting for transfers between devices, from_everyone(): return lax.all_to_all(copies, axis, split_axis=0, concat_axis=0, tiled=True)  46.1 us
    all_to_all x11, starting transfers between devices, from_everyone(): return lax.all_to_all(copies, axis, split_axis=0, concat_axis=0, tiled=True)  42.7 us
  transfers between devices with their start and end apart: 22, of which 18 were waited for; matrix products, arithmetic and copies ran while one was open for 17% of the time, Pallas kernels for 0%

commit v1 on v0

--- a/solution.py
+++ b/solution.py
@@ -7,6 +7,11 @@
 EPS = 1e-06
 
 
+def gather_over(array, axis, dim):
+    sent = jnp.stack([array] * lax.axis_size(axis))
+    return jnp.concatenate(lax.all_to_all(sent, axis, 0, 0), axis=dim)
+
+
 def from_everyone(value, axis):
     copies = jnp.broadcast_to(value, (lax.axis_size(axis), *value.shape))
     return lax.all_to_all(copies, axis, split_axis=0, concat_axis=0, tiled=True)
@@ -48,7 +53,7 @@
     turned = [jnp.moveaxis(a, dim, 0) for a, dim in zip(arrays, dims)]
     widths = [t[0].size for t in turned]
     both = jnp.concatenate([t.reshape(-1, w) for t, w in zip(turned, widths)], axis=1)
-    out = lax.all_gather(both, axis, axis=0, tiled=True)
+    out = gather_over(both, axis, 0)
     blocks = jnp.split(out, [sum(widths[:k]) for k in range(1, len(widths))], axis=1)
     return tuple(
         (

time: 829 us -> 1080 us (1.30)
  waiting for transfers between devices: 366 us -> 570 us
  starting transfers between devices: 66.1 us -> 121 us
  blocking collectives: 132 us -> 111 us
  local copies, waits for them, and re-layouts: 117 us -> 130 us
    all_to_all x0 -> x1, waiting for transfers between devices: none -> 262 us  [gather_over(): return jnp.concatenate(lax.all_to_all(sent, axis, 0, 0), axis=dim)]
    all_gather x1 -> x0, waiting for transfers between devices: 52.9 us -> none  [gather_turned(): out = lax.all_gather(both, axis, axis=0, tiled=True)]
    ppermute x4, starting transfers between devices: 6.16 us -> 33.5 us  [from_behind(): return lax.ppermute(value, axis, pairs)]
    all_to_all x11, starting transfers between devices: 42.7 us -> 62.6 us  [from_everyone(): return lax.all_to_all(copies, axis, split_axis=0, concat_axis=0, tiled=True)]
    all_to_all x4, blocking collectives: 76.1 us -> 56.7 us  [sent_and_summed(): lax.all_to_all(cut_along(value, dim, peers), axis, 0, 0, tiled=True)]
    ppermute x4, waiting for transfers between devices: 0.94 us -> 12.2 us  [from_behind(): return lax.ppermute(value, axis, pairs)]
    split x9 -> x7, local copies, waits for them, and re-layouts: 24.6 us -> 28.9 us  [gather_turned(): jnp.split(out, [sum(widths[:k]) for k in range(1, len(widths))], axis=1)]
    unnamed x4 -> x3, waiting for transfers between devices: 110 us -> 110 us
  transfers between devices with their start and end apart: 22 -> 22, of which waited for: 18 -> 18; matrix products, arithmetic and copies ran while one was open for 17% -> 14% of each run, Pallas kernels for 0% -> 0%
where the time goes in v1:
time: 1080 us; the launch traced here: 1070 us
  waiting for transfers between devices  570 us (53%)
  local copies, waits for them, and re-layouts  130 us (12%)
  starting transfers between devices  121 us (11%)
  blocking collectives  111 us (10%)
  matrix products  64.8 us (6%)
  other arithmetic  56.5 us (5%)
  between operations  16.8 us (2%)
    all_to_all x1, waiting for transfers between devices, gather_over(): return jnp.concatenate(lax.all_to_all(sent, axis, 0, 0), axis=dim)  262 us
    reduce_scatter x1, waiting for transfers between devices, per_device(): summed = lax.psum_scatter(stacked, 'seq', scatter_dimension=2, tiled=True)  121 us
    unnamed x3, waiting for transfers between devices  110 us
    all_to_all x11, starting transfers between devices, from_everyone(): return lax.all_to_all(copies, axis, split_axis=0, concat_axis=0, tiled=True)  62.6 us
    all_to_all x4, blocking collectives, sent_and_summed(): lax.all_to_all(cut_along(value, dim, peers), axis, 0, 0, tiled=True)  56.7 us
    all_to_all x6, blocking collectives, from_everyone(): return lax.all_to_all(copies, axis, split_axis=0, concat_axis=0, tiled=True)  54.7 us
    dot_general x24, matrix products, bdot(): return jnp.dot(left, right, preferred_element_type=jnp.float32)  54.6 us
    all_to_all x11, waiting for transfers between devices, from_everyone(): return lax.all_to_all(copies, axis, split_axis=0, concat_axis=0, tiled=True)  39.4 us
  transfers between devices with their start and end apart: 22, of which 18 were waited for; matrix products, arithmetic and copies ran while one was open for 14% of the time, Pallas kernels for 0%

profile of v1, /device:TPU:0, one launch (start us, length us, event | category | flops | bytes accessed | tf_op | source)
XLA Modules:
  0.0 1070.7 jit_solution(4597683827903787434)
XLA Ops:
  8.9 5.4 all-to-all-start.1
  25.5 8.9 all-to-all-done.2
  34.4 6.7 stack.181
  41.1 7.6 all-to-all-start
  50.3 261.9 %all-to-all-done = bf16[32,32,8960]{2,1,0:T(8,128)(2,1)} async-done(((bf16[32,32,8960]{2,1,0:T(8,128)(2,1)}), bf16[32,32,8960]{2,1,0:T(8,128)(2,1)}, u32[]{:S(2)}, u32[]{:S(2)}) %all-to-all-start) | async-done | bytes 18350112 | tf_op jit(solution)/shard_map/all_to_all | solution.py:12
  335.0 13.3 %all_to_all.139 = f32[4,256,256]{2,1,0:T(8,128)S(1)} all-to-all(f32[4,256,256]{2,1,0:T(8,128)S(1)} %convolution_bitcast_fusion.16), channel_id=1, replica_groups=mesh['seq'=32,'tp'=4] {'tp'}, dimensions={0} | all-to-all | bytes 2097152 | tf_op jit(solution)/shard_map/all_to_all | solution.py:42
  352.4 7.9 split.18
  365.1 13.0 %reshape.246 = bf16[1024,2,2,1152]{3,2,1,0:T(2,128)(2,1)} reshape(bf16[1024,4608]{1,0:T(8,128)(2,1)} %split.18) | data formatting | bytes 18874368 | tf_op jit(solution)/shard_map/reshape | solution.py:60
  378.2 8.5 copy.486
  386.7 6.7 copy.396
  414.8 15.9 %all_to_all.140 = f32[4,256,256]{2,1,0:T(8,128)S(1)} all-to-all(f32[4,256,256]{2,1,0:T(8,128)S(1)} %convolution_bitcast_fusion.15), channel_id=1, replica_groups=mesh['seq'=32,'tp'=4] {'tp'}, dimensions={0} | all-to-all | bytes 2097152 | tf_op jit(solution)/shard_map/all_to_all | solution.py:42
  430.9 7.6 all_to_all.141
  438.7 10.5 all_to_all.142
  452.3 29.5 %collective-permute-start.1 = (f32[2,256]{1,0:T(2,128)S(1)}, f32[2,256]{1,0:T(2,128)S(1)}, u32[]{:S(2)}, u32[]{:S(2)}) collective-permute-start(f32[2,256]{1,0:T(2,128)S(1)} %slice.242), channel_id=1, source_target_pairs={{0,4},{4,8},{8,12},{12,16},{16,20},{20,24},{24,28},{28,32},{32,36}... | collective-permute-start | bytes 6152 | tf_op jit(solution)/shard_map/ppermute | solution.py:49
  484.0 13.3 %all_to_all.143 = f32[4,256,256]{2,1,0:T(8,128)S(1)} all-to-all(f32[4,256,256]{2,1,0:T(8,128)S(1)} %convolution_bitcast_fusion.14), channel_id=1, replica_groups=mesh['seq'=32,'tp'=4] {'tp'}, dimensions={0} | all-to-all | bytes 2097152 | tf_op jit(solution)/shard_map/all_to_all | solution.py:42
  497.5 7.7 all_to_all.144
  510.0 7.9 all-to-all-done.11
  562.0 9.0 all-to-all-done.12
  582.3 10.5 all_to_all.145
  602.2 14.2 %all_to_all.146 = f32[4,256,256]{2,1,0:T(8,128)} all-to-all(f32[4,256,256]{2,1,0:T(8,128)S(1)} %convolution_bitcast_fusion.10), channel_id=1, replica_groups=mesh['seq'=32,'tp'=4] {'tp'}, dimensions={0} | all-to-all | bytes 2097152 | tf_op jit(solution)/shard_map/all_to_all | solution.py:42
  618.4 7.7 all_to_all.147
  627.8 10.6 all_to_all.148
  680.6 9.4 pad_maximum_fusion.1
  690.0 14.9 %copy.421 = f32[2,1152,1024]{1,0,2:T(2,128)} copy(f32[2,1152,1024]{2,1,0:T(8,128)} %pad_maximum_fusion.1) | data formatting | bytes 18874368 | tf_op jit(solution)/shard_map/stack | solution.py:279
  712.2 8.8 collective-permute-done.3
  726.9 10.3 copy.419
  751.0 6.7 pad_maximum_fusion
  767.0 9.5 all-to-all-done.23
  787.0 24.2 %all-to-all-start.25 = ((f32[32,1,2560]{2,1,0:T(1,128)}), f32[32,1,2560]{2,1,0:T(1,128)S(1)}, u32[]{:S(2)}, u32[]{:S(2)}) async-start(f32[32,1,2560]{2,1,0:T(1,128)} %broadcast_in_dim.75), calls=%async_computation.26 | async-start | bytes 655360 | tf_op jit(solution)/shard_map/all_to_all | solution.py:17
  812.2 9.7 all-to-all-done.25
  825.2 109.6 %all-reduce.12.cloned.1.call-done = (f32[2,3,1024,256]{3,0,1,2:T(2,128)}, f32[2,256,1024]{1,0,2:T(2,128)}, f32[2,1152,1024]{1,0,2:T(2,128)}) async-done(((f32[2,3,1024,256]{3,0,1,2:T(2,128)}, f32[2,256,1024]{1,0,2:T(2,128)}, f32[2,1152,1024]{1,0,2:T(2,128)}), (f32[2,3,1024,256]{3,0,1,2:T(2,128)}, f32[2,256,1024]{1,0,2:T(2,128)}, f32[2,1152,1024]{1,0,2:T(2,128)})) %all-reduce.12.cloned.1.call-update) | async-done | bytes 17825808
  940.4 120.7 %reduce-scatter.2.cloned.1.call-done = f32[2,2,32,1152]{3,2,1,0:T(8,128)} async-done(((f32[2,2,1024,1152]{3,2,1,0:T(8,128)}), f32[2,2,32,1152]{3,2,1,0:T(8,128)}) %reduce-scatter.2.cloned.1.call-update) | async-done | bytes 589840 | tf_op jit(solution)/shard_map/reduce_scatter | solution.py:281
  (410 shorter events, 245.8 us)
Async XLA Ops:
  8.9 10.7 %all-to-all-start.1 = ((f32[4,1,256]{2,1,0:T(1,128)}), f32[4,1,256]{2,1,0:T(1,128)S(1)}, u32[]{:S(2)}, u32[]{:S(2)}) async-start(f32[4,1,256]{2,1,0:T(1,128)} %broadcast_in_dim.59), calls=%async_computation.1 | async-start | bytes 8192 | tf_op jit(solution)/shard_map/all_to_all | solution.py:17
  19.0 374.4 %copy-start.75 = (f32[1,1,256]{2,1,0:T(1,128)}, f32[1,1,256]{2,1,0:T(1,128)S(1)}, u32[]{:S(2)}) copy-start(f32[1,1,256]{2,1,0:T(1,128)S(1)} %get-tuple-element.296) | copy-start | bytes 3076
  19.0 598.7 %copy-start.77 = (f32[1,1,256]{2,1,0:T(1,128)}, f32[1,1,256]{2,1,0:T(1,128)S(1)}, u32[]{:S(2)}) copy-start(f32[1,1,256]{2,1,0:T(1,128)S(1)} %get-tuple-element.295) | copy-start | bytes 3076
  20.7 13.7 %all-to-all-start.2 = ((bf16[4,256,256]{2,1,0:T(8,128)(2,1)}), bf16[4,256,256]{2,1,0:T(8,128)(2,1)S(1)}, u32[]{:S(2)}, u32[]{:S(2)}) async-start(bf16[4,256,256]{2,1,0:T(8,128)(2,1)} %broadcast_in_dim.60), calls=%async_computation.2 | async-start | bytes 1048576 | tf_op jit(solution)/shard_map/all_to_all | solution.py:17
  41.1 271.1 %all-to-all-start = ((bf16[32,32,8960]{2,1,0:T(8,128)(2,1)}), bf16[32,32,8960]{2,1,0:T(8,128)(2,1)}, u32[]{:S(2)}, u32[]{:S(2)}) async-start(bf16[32,32,8960]{2,1,0:T(8,128)(2,1)} %stack.181), calls=%async_computation | async-start | bytes 36700160 | tf_op jit(solution)/shard_map/all_to_all | solution.py:12
  48.7 283.5 %copy-start.78 = (f32[1,1,256]{2,0,1:T(1,128)}, f32[1,1,256]{2,0,1:T(1,128)S(1)}, u32[]{:S(2)}) copy-start(f32[1,1,256]{2,0,1:T(1,128)S(1)} %get-tuple-element.290) | copy-start | bytes 3076
  48.7 283.5 %copy-start.80 = (f32[1,1,256]{2,0,1:T(1,128)}, f32[1,1,256]{2,0,1:T(1,128)S(1)}, u32[]{:S(2)}) copy-start(f32[1,1,256]{2,0,1:T(1,128)S(1)} %get-tuple-element.291) | copy-start | bytes 3076
  48.7 283.5 %copy-start.82 = (f32[1,1,256]{2,0,1:T(1,128)}, f32[1,1,256]{2,0,1:T(1,128)S(1)}, u32[]{:S(2)}) copy-start(f32[1,1,256]{2,0,1:T(1,128)S(1)} %get-tuple-element.292) | copy-start | bytes 3076
  326.3 5.9 collective-permute-start
  349.1 44.2 %all-to-all-start.4 = ((f32[4,1,256]{2,1,0:T(1,128)}), f32[4,1,256]{2,1,0:T(1,128)S(1)}, u32[]{:S(2)}, u32[]{:S(2)}) async-start(f32[4,1,256]{2,1,0:T(1,128)} %broadcast_in_dim.61), calls=%async_computation.4 | async-start | bytes 8192 | tf_op jit(solution)/shard_map/all_to_all | solution.py:17
  394.5 12.8 %all-to-all-start.5 = ((bf16[4,256,256]{1,2,0:T(8,128)(2,1)}), bf16[4,256,256]{1,2,0:T(8,128)(2,1)S(1)}, u32[]{:S(2)}, u32[]{:S(2)}) async-start(bf16[4,256,256]{1,2,0:T(8,128)(2,1)} %broadcast_in_dim.62), calls=%async_computation.5 | async-start | bytes 1048576 | tf_op jit(solution)/shard_map/all_to_all | solution.py:17
  452.3 30.3 %collective-permute-start.1 = (f32[2,256]{1,0:T(2,128)S(1)}, f32[2,256]{1,0:T(2,128)S(1)}, u32[]{:S(2)}, u32[]{:S(2)}) collective-permute-start(f32[2,256]{1,0:T(2,128)S(1)} %slice.242), channel_id=1, source_target_pairs={{0,4},{4,8},{8,12},{12,16},{16,20},{20,24},{24,28},{28,32},{32,36}... | collective-permute-start | bytes 6152 | tf_op jit(solution)/shard_map/ppermute | solution.py:49
  506.3 11.5 %all-to-all-start.11 = ((bf16[4,256,256]{1,2,0:T(8,128)(2,1)}), bf16[4,256,256]{1,2,0:T(8,128)(2,1)S(1)}, u32[]{:S(2)}, u32[]{:S(2)}) async-start(bf16[4,256,256]{1,2,0:T(8,128)(2,1)} %broadcast_in_dim.66), calls=%async_computation.11 | async-start | bytes 1048576 | tf_op jit(solution)/shard_map/all_to_all | solution.py:17
  518.7 11.5 %all-to-all-start.13 = ((bf16[4,256,256]{1,2,0:T(8,128)(2,1)}), bf16[4,256,256]{1,2,0:T(8,128)(2,1)S(1)}, u32[]{:S(2)}, u32[]{:S(2)}) async-start(bf16[4,256,256]{1,2,0:T(8,128)(2,1)} %broadcast_in_dim.67), calls=%async_computation.13 | async-start | bytes 1048576 | tf_op jit(solution)/shard_map/all_to_all | solution.py:17
  541.2 15.2 %all-to-all-start.14 = ((f32[4,256,256]{2,1,0:T(8,128)}), f32[4,256,256]{2,1,0:T(8,128)}, u32[]{:S(2)}, u32[]{:S(2)}) async-start(f32[4,256,256]{2,1,0:T(8,128)} %bitcast.335), calls=%async_computation.14 | async-start | bytes 2097152 | tf_op jit(solution)/shard_map/all_to_all | solution.py:42
  556.4 14.6 %all-to-all-start.12 = ((f32[4,256,256]{2,1,0:T(8,128)}), f32[4,256,256]{2,1,0:T(8,128)S(1)}, u32[]{:S(2)}, u32[]{:S(2)}) async-start(f32[4,256,256]{2,1,0:T(8,128)} %convolution_bitcast_fusion.13), calls=%async_computation.12 | async-start | bytes 2097152 | tf_op jit(solution)/shard_map/all_to_all | solution.py:42
  571.6 8.5 all-to-all-start.15
  595.2 5.6 collective-permute-start.2
  648.9 15.2 %all-to-all-start.20 = ((f32[4,256,256]{2,1,0:T(8,128)}), f32[4,256,256]{2,1,0:T(8,128)}, u32[]{:S(2)}, u32[]{:S(2)}) async-start(f32[4,256,256]{2,1,0:T(8,128)} %bitcast.370), calls=%async_computation.20 | async-start | bytes 2097152 | tf_op jit(solution)/shard_map/all_to_all | solution.py:42
  666.8 8.5 all-to-all-start.21
  677.1 27.8 %all-to-all-start.22 = ((bf16[4,256,256]{1,2,0:T(8,128)(2,1)}), bf16[4,256,256]{1,2,0:T(8,128)(2,1)S(1)}, u32[]{:S(2)}, u32[]{:S(2)}) async-start(bf16[4,256,256]{1,2,0:T(8,128)(2,1)} %broadcast_in_dim.73), calls=%async_computation.22 | async-start | bytes 1048576 | tf_op jit(solution)/shard_map/all_to_all | solution.py:17
  680.6 254.2 %all-reduce.12.cloned.1.call-start = ((), (), s32[]{:S(2)}) async-start(), calls=%async_computation.28 | async-start | bytes 35651584
  708.3 12.7 %collective-permute-start.3 = (f32[2,256]{1,0:T(2,128)}, f32[2,256]{1,0:T(2,128)}, u32[]{:S(2)}, u32[]{:S(2)}) collective-permute-start(f32[2,256]{1,0:T(2,128)} %slice.252), channel_id=1, source_target_pairs={{4,0},{8,4},{12,8},{16,12},{20,16},{24,20},{28,24},{32,28},{36,32}... | collective-permute-start | bytes 6152 | tf_op jit(solution)/shard_map/ppermute | solution.py:49
  737.3 323.8 %reduce-scatter.2.cloned.1.call-start = ((), (), s32[]{:S(2)}) async-start(), calls=%async_computation.27 | async-start | bytes 19464192 | tf_op jit(solution)/shard_map/reduce_scatter | solution.py:281
  760.9 15.6 %all-to-all-start.23 = ((f32[4,256,256]{2,1,0:T(8,128)}), f32[4,256,256]{2,1,0:T(8,128)S(1)}, u32[]{:S(2)}, u32[]{:S(2)}) async-start(f32[4,256,256]{2,1,0:T(8,128)} %convolution_bitcast_fusion.9), calls=%async_computation.23 | async-start | bytes 2097152 | tf_op jit(solution)/shard_map/all_to_all | solution.py:42
  776.6 161.0 %copy-start.63 = (f32[2,256,32]{1,2,0:T(8,128)S(1)}, f32[2,256,32]{1,2,0:T(8,128)}, u32[]{:S(2)}) copy-start(f32[2,256,32]{1,2,0:T(8,128)} %param.23) | copy-start | bytes 196612
  776.6 161.0 %copy-start.66 = (f32[2,256,32]{1,2,0:T(8,128)S(1)}, f32[2,256,32]{1,2,0:T(8,128)}, u32[]{:S(2)}) copy-start(f32[2,256,32]{1,2,0:T(8,128)} %param.30) | copy-start | bytes 196612
  776.6 161.7 %copy-start.48 = (f32[2,3,32,256]{3,2,1,0:T(8,128)S(1)}, f32[2,3,32,256]{3,2,1,0:T(8,128)}, u32[]{:S(2)}) copy-start(f32[2,3,32,256]{3,2,1,0:T(8,128)} %param.22) | copy-start | bytes 589828
  776.6 161.7 %copy-start.64 = (f32[2,3,32,256]{3,2,1,0:T(8,128)S(1)}, f32[2,3,32,256]{3,2,1,0:T(8,128)}, u32[]{:S(2)}) copy-start(f32[2,3,32,256]{3,2,1,0:T(8,128)} %param.28) | copy-start | bytes 589828
  776.7 161.7 %copy-start.65 = (f32[2,3,32,256]{3,2,1,0:T(8,128)S(1)}, f32[2,3,32,256]{3,2,1,0:T(8,128)}, u32[]{:S(2)}) copy-start(f32[2,3,32,256]{3,2,1,0:T(8,128)} %param.29) | copy-start | bytes 589828
  777.5 8.6 all-to-all-start.24
  787.0 34.8 %all-to-all-start.25 = ((f32[32,1,2560]{2,1,0:T(1,128)}), f32[32,1,2560]{2,1,0:T(1,128)S(1)}, u32[]{:S(2)}, u32[]{:S(2)}) async-start(f32[32,1,2560]{2,1,0:T(1,128)} %broadcast_in_dim.75), calls=%async_computation.26 | async-start | bytes 655360 | tf_op jit(solution)/shard_map/all_to_all | solution.py:17
  (92 other events, 2180.1 us)
Sparse Core Ops, SparseCore 0:
  737.4 197.3 all-reduce.11
  939.4 121.6 reduce-scatter.1
